TPU v7x, 32 devices: a whole 2x2x4 slice. The times are simulated.
32 devices in a mesh: tm: 4 (over y, x), pts: 8 (over z, core).
Axes of the slice: x: 2, y: 2, z: 4, core: 2. Of those that a mesh axis runs over, the one named last changes fastest.
Arguments:
- orbitals: bfloat16 [8192, 2048], P('pts'), may hold values from -6 to 6
- panel_orbitals: bfloat16 [1024, 2048], P(('tm', 'pts')), may hold values from -0.1796875 to 0.1796875
- band_gap: float32 [2048], replicated, may hold values from 0.1 to 1
- tau_points: float32 [4], replicated, may hold values from 0.1 to 2
- quad_weight: float32 [4], replicated, may hold values from 0.1 to 1
- frequencies: float32 [8], replicated, may hold values from 0.1 to 3
- coulomb: bfloat16 [1024, 1024], P(('tm', 'pts')), may hold values from -0.1875 to 0.1875
Outputs:
- screened: bfloat16 [8, 8192, 1024], P(None, ('pts', 'tm'))
All inputs are finite; a program needn't handle non-finite values.
Results may differ from a plain program's by a relative error of at most 0.0056.
Values may be sent and summed in bfloat16 or wider, within the bound.
A program may use at most 64 MiB of HBM per device.

v0:
```python
import jax
import jax.numpy as jnp
from jax import lax
from jax.sharding import PartitionSpec as P

NOCC = 512
PANEL = 1024
TAU_DEV = 1
FREQS = 8


def contract(left, right):
    return lax.dot_general(
        left, right, (((1,), (1,)), ((), ())), preferred_element_type=jnp.float32
    )


def shards(orbitals, panel_orbitals, band_gap, tau_points, quad_weight, frequencies, coulomb):
    group = lax.axis_index("tm")
    own_taus = lax.dynamic_slice_in_dim(tau_points, group * TAU_DEV, TAU_DEV)
    decay = jnp.exp(-band_gap[None, :] * own_taus[:, None])
    occ_rows = orbitals[:, :NOCC]
    vir_rows = orbitals[:, NOCC:]
    widened = lax.all_gather(panel_orbitals, ("tm", "pts"), axis=0, tiled=True).astype(jnp.float32)
    scaled = (widened * decay[0][None, :]).astype(jnp.bfloat16)
    green_occ = contract(occ_rows, scaled[:, :NOCC])
    green_vir = contract(vir_rows, scaled[:, NOCC:])
    layers = [(-(green_occ * green_vir)).astype(jnp.bfloat16)]
    polar = jnp.stack(layers)
    regrouped = lax.all_to_all(polar, "tm", split_axis=1, concat_axis=0, tiled=True)
    times_all = regrouped.shape[0]
    row_count = regrouped.shape[1]
    cosines = quad_weight[None, :] * jnp.cos(frequencies[:, None] * tau_points[None, :])
    flat = regrouped.reshape(times_all, row_count * PANEL).astype(jnp.float32)
    transformed = jnp.dot(cosines, flat, precision=lax.Precision.HIGHEST).astype(jnp.bfloat16)
    transformed = transformed.reshape(FREQS * row_count, PANEL)
    whole_block = lax.all_gather(coulomb, ("tm", "pts"), axis=0, tiled=True)
    screened = jnp.dot(transformed, whole_block, preferred_element_type=jnp.float32)
    return screened.astype(jnp.bfloat16).reshape(FREQS, row_count, PANEL)


def solution(mesh):
    placed = (P("pts", None), P(("tm", "pts"), None), P(), P(), P(), P(), P(("tm", "pts"), None))
    return jax.shard_map(
        shards, mesh=mesh, in_specs=placed, out_specs=P(None, ("pts", "tm"), None), check_vma=False
    )
```

profile of v0, /device:TPU:0, one launch (start us, length us, event | category | flops | bytes accessed | tf_op | source)
XLA Modules:
  0.0 188.5 jit_solution(1147528016978019313)
XLA Ops:
  6.5 0.0 all-gather.3.cloned.1.call-start
  6.5 0.7 all-gather.3.cloned.1.call-update
  7.3 0.0 all-gather.5.cloned.1.call-start
  7.3 0.7 all-gather.5.cloned.1.call-update
  8.0 1.2 dynamic_slice.3
  9.3 1.3 multiply_exponential_fusion
  10.6 64.2 %all-gather.3.cloned.1.call-done = bf16[1024,2048]{1,0:T(8,128)(2,1)} async-done(((bf16[32,2048]{1,0:T(8,128)(2,1)}), bf16[1024,2048]{1,0:T(8,128)(2,1)}) %all-gather.3.cloned.1.call-update) | async-done | bytes 4194320 | tf_op jit(solution)/shard_map/all_gather | solution.py:24
  74.8 0.0 copy-start
  74.8 3.4 %multiply_convert_fusion = bf16[1024,2048]{1,0:T(8,128)(2,1)S(1)} fusion(bf16[1024,2048]{1,0:T(8,128)(2,1)} %all-gather.3.cloned.1.call-done, f32[2048]{0:T(1024)S(1)} %multiply_exponential_fusion), kind=kLoop, calls=%fused_computation.1 | loop fusion | flops 6291456 | bytes 8396800 | tf_op jit(solution)/shard_map/convert_element_type | solution.py:25
  78.2 0.0 copy-done
  78.2 3.5 %fusion = f32[1024,1024]{1,0:T(8,128)S(1)} fusion(bf16[1024,2048]{1,0:T(8,128)(2,1)S(1)} %multiply_convert_fusion, bf16[1024,2048]{1,0:T(8,128)(2,1)S(1)} %copy-done), kind=kOutput, calls=%fused_computation.4 | convolution fusion | flops 3221225472 | bytes 10485760 | tf_op jit(solution)/shard_map/dot_general | solution.py:13
  81.7 1.3 fusion.3
  83.0 7.5 %copy.9 = bf16[1,1024,1024]{2,0,1:T(2,128)(2,1)} copy(bf16[1,1024,1024]{1,2,0:T(8,128)(2,1)S(1)} %fusion.3) | data formatting | bytes 4194304 | tf_op jit(solution)/shard_map/stack | solution.py:29
  90.5 0.5 broadcast.7
  91.1 12.8 %reduce.2 = bf16[1024,1024]{1,0:T(8,128)(2,1)S(1)} reduce(bf16[1024,1,1024]{2,1,0:T(2,128)(2,1)} %bitcast.12, bf16[]{:T(256)} %broadcast.7), dimensions={1}, to_apply=%bitcast.6.reduce_sub_computation | reduce | bytes 4194306
  103.8 2.8 %reshape.27 = bf16[4,2,131072]{2,1,0:T(2,128)(2,1)} reshape(bf16[1024,1024]{1,0:T(8,128)(2,1)S(1)} %reduce.2) | data formatting | bytes 4194304
  106.6 33.3 %all_to_all.4 = bf16[4,2,131072]{2,1,0:T(2,128)(2,1)S(1)} all-to-all(bf16[4,2,131072]{2,1,0:T(2,128)(2,1)} %reshape.27), channel_id=1, replica_groups=mesh['tm'=4,'pts'=8] {'tm'}, dimensions={0} | all-to-all | bytes 4194304 | tf_op jit(solution)/shard_map/all_to_all | solution.py:30
  139.9 3.3 %reshape.28 = bf16[1024,1,1024]{2,1,0:T(2,128)(2,1)} reshape(bf16[4,2,131072]{2,1,0:T(2,128)(2,1)S(1)} %all_to_all.4) | data formatting | bytes 4194304
  143.2 0.0 copy-start.1
  143.2 0.0 copy-start.2
  143.2 0.0 copy-start.3
  143.2 14.7 %bitcast_reduce_fusion = bf16[1024,1024]{1,0:T(8,128)(2,1)} fusion(bf16[1024,1,1024]{2,1,0:T(2,128)(2,1)} %reshape.28), kind=kLoop, calls=%fused_computation.17 | loop fusion | bytes 4194304 | tf_op jit(solution)/shard_map/all_to_all | solution.py:30
  157.9 3.2 %reshape.23 = bf16[4,262144]{1,0:T(4,128)(2,1)S(1)} reshape(bf16[1024,1024]{1,0:T(8,128)(2,1)} %bitcast_reduce_fusion) | data formatting | bytes 4194304 | tf_op jit(solution)/shard_map/reshape | solution.py:34
  161.1 0.0 copy-done.1
  161.1 0.0 copy-done.2
  161.1 0.0 copy-done.3
  161.1 5.1 %convolution_convert_fusion = bf16[8,262144]{1,0:T(8,128)(2,1)} fusion(bf16[4,262144]{1,0:T(4,128)(2,1)S(1)} %reshape.23, f32[4]{0:T(128)S(1)} %copy-done.1, f32[8]{0:T(128)S(1)} %copy-done.2, f32[4]{0:T(128)S(1)} %copy-done.3), kind=kOutput, calls=%fused_computation | convolution fusion | flops 102760512 | bytes 6291520 | tf_op jit(solution)/shard_map/dot_general | solution.py:35
  166.2 6.0 %reshape.24 = bf16[2048,1024]{1,0:T(8,128)(2,1)} reshape(bf16[8,262144]{1,0:T(8,128)(2,1)} %convolution_convert_fusion) | data formatting | bytes 8388608 | tf_op jit(solution)/shard_map/reshape | solution.py:36
  172.2 0.0 all-gather.5.cloned.1.call-done
  172.2 9.4 %convolution_convert_fusion.1 = bf16[2048,1024]{1,0:T(8,128)(2,1)} fusion(bf16[2048,1024]{1,0:T(8,128)(2,1)} %reshape.24, bf16[1024,1024]{1,0:T(8,128)(2,1)} %all-gather.5.cloned.1.call-done), kind=kOutput, calls=%fused_computation.3 | convolution fusion | flops 4297064448 | bytes 10485760 | tf_op jit(solution)/shard_map/dot_general | solution.py:38
Async XLA Ops:
  6.5 68.2 %all-gather.3.cloned.1.call-start = ((), (), s32[]{:S(2)}) async-start(), calls=%async_computation.1 | async-start | bytes 4325376 | tf_op jit(solution)/shard_map/all_gather | solution.py:24
  7.3 165.0 %all-gather.5.cloned.1.call-start = ((), (), s32[]{:S(2)}) async-start(), calls=%async_computation.2 | async-start | bytes 2162688 | tf_op jit(solution)/shard_map/all_gather | solution.py:37
  74.8 3.5 %copy-start = (bf16[1024,2048]{1,0:T(8,128)(2,1)S(1)}, bf16[1024,2048]{1,0:T(8,128)(2,1)}, u32[]{:S(2)}) copy-start(bf16[1024,2048]{1,0:T(8,128)(2,1)} %param.7) | copy-start | bytes 12582916
  143.2 17.9 %copy-start.1 = (f32[4]{0:T(128)S(1)}, f32[4]{0:T(128)}, u32[]{:S(2)}) copy-start(f32[4]{0:T(128)} %param.10) | copy-start | bytes 52
  143.2 17.9 %copy-start.2 = (f32[8]{0:T(128)S(1)}, f32[8]{0:T(128)}, u32[]{:S(2)}) copy-start(f32[8]{0:T(128)} %param.12) | copy-start | bytes 100
  143.2 17.9 %copy-start.3 = (f32[4]{0:T(128)S(1)}, f32[4]{0:T(128)}, u32[]{:S(2)}) copy-start(f32[4]{0:T(128)} %param.11) | copy-start | bytes 52
Sparse Core Ops, SparseCore 0:
  10.3 64.3 all-gather.2
  77.7 60.9 all-gather.4
where the time goes:
time: 189 us; the launch traced here: 188 us
  waiting for transfers between devices  65.6 us (35%)
  local copies, waits for them, and re-layouts  39.2 us (21%)
  blocking collectives  33.3 us (18%)
  matrix products  19.3 us (10%)
  other arithmetic  17.5 us (9%)
  between operations  13.5 us (7%)
    all_gather x1, waiting for transfers between devices, shards(): lax.all_gather(panel_orbitals, ('tm', 'pts'), axis=0, tiled=True)  64.2 us
    all_to_all x1, blocking collectives, shards(): lax.all_to_all(polar, 'tm', split_axis=1, concat_axis=0, tiled=True)  33.3 us
    all_to_all x1, local copies, waits for them, and re-layouts, shards(): lax.all_to_all(polar, 'tm', split_axis=1, concat_axis=0, tiled=True)  14.7 us
    unnamed x1, other arithmetic  12.8 us
    dot_general x1, matrix products, shards(): jnp.dot(transformed, whole_block, preferred_element_type=jnp.float32)  9.41 us
    another operation x1, local copies, waits for them, and re-layouts, shards(): polar = jnp.stack(layers)  7.52 us
    unnamed x11, local copies, waits for them, and re-layouts  6.57 us
    reshape x1, local copies, waits for them, and re-layouts, shards(): transformed = transformed.reshape(FREQS * row_count, PANEL)  6.02 us
  transfers between devices with their start and end apart: 2, of which 1 were waited for; matrix products, arithmetic and copies ran while one was open for 35% of the time, Pallas kernels for 0%

commit v1 on v0

--- a/solution.py
+++ b/solution.py
@@ -27,7 +27,9 @@
     green_vir = contract(vir_rows, scaled[:, NOCC:])
     layers = [(-(green_occ * green_vir)).astype(jnp.bfloat16)]
     polar = jnp.stack(layers)
-    regrouped = lax.all_to_all(polar, "tm", split_axis=1, concat_axis=0, tiled=True)
+    regrouped = jnp.concatenate(
+        lax.all_to_all(jnp.stack(jnp.split(polar, lax.axis_size("tm"), axis=1)), "tm", 0, 0), axis=0
+    )
     times_all = regrouped.shape[0]
     row_count = regrouped.shape[1]
     cosines = quad_weight[None, :] * jnp.cos(frequencies[:, None] * tau_points[None, :])

time: 189 us -> 151 us (0.80)
  local copies, waits for them, and re-layouts: 39.2 us -> 13 us
  other arithmetic: 17.5 us -> 5.05 us
  waiting for transfers between devices: 65.6 us -> 69.6 us
  blocking collectives: 33.3 us -> 30.4 us
    unnamed x1 -> x0, other arithmetic: 12.8 us -> none
    all_to_all x1, local copies, waits for them, and re-layouts: 14.7 us -> 2.37 us  [shards(): lax.all_to_all(jnp.stack(jnp.split(polar, lax.axis_size('tm'), axis=1)),...]
    another operation x1, local copies, waits for them, and re-layouts: 7.52 us -> 0.14 us  [shards(): jnp.stack(jnp.split(polar, lax.axis_size('tm'), axis=1))]
    all_gather x1, waiting for transfers between devices: 0.01 us -> 4.07 us  [shards(): whole_block = lax.all_gather(coulomb, ('tm', 'pts'), axis=0, tiled=True)]
    unnamed x11 -> x9, local copies, waits for them, and re-layouts: 6.57 us -> 3.23 us
    reshape x1 -> x0, local copies, waits for them, and re-layouts: 3.2 us -> none  [shards(): flat = regrouped.reshape(times_all, row_count * PANEL).astype(jnp.float32)]
    all_to_all x1, blocking collectives: 33.3 us -> 30.4 us  [shards(): lax.all_to_all(jnp.stack(jnp.split(polar, lax.axis_size('tm'), axis=1)),...]
  transfers between devices with their start and end apart: 2 -> 2, of which waited for: 1 -> 2; matrix products, arithmetic and copies ran while one was open for 35% -> 19% of each run, Pallas kernels for 0% -> 0%
where the time goes in v1:
time: 151 us
  waiting for transfers between devices  69.6 us (46%)
  blocking collectives  30.4 us (20%)
  matrix products  19.3 us (13%)
  between operations  13.5 us (9%)
  local copies, waits for them, and re-layouts  13 us (9%)
  other arithmetic  5.05 us (3%)
    all_gather x1, waiting for transfers between devices, shards(): lax.all_gather(panel_orbitals, ('tm', 'pts'), axis=0, tiled=True)  64.2 us
    all_to_all x1, blocking collectives, shards(): lax.all_to_all(jnp.stack(jnp.split(polar, lax.axis_size('tm'), axis=1)),...  30.4 us
    dot_general x1, matrix products, shards(): jnp.dot(transformed, whole_block, preferred_element_type=jnp.float32)  9.41 us
    reshape x1, local copies, waits for them, and re-layouts, shards(): transformed = transformed.reshape(FREQS * row_count, PANEL)  6.04 us
    dot_general x1, matrix products, shards(): jnp.dot(cosines, flat, precision=lax.Precision.HIGHEST).astype(jnp.bfloat16)  5.12 us
    dot_general x2, matrix products, contract(): lax.dot_general(left, right, (((1,), (1,)), ((), ())), preferred_element_...  4.78 us
    all_gather x1, waiting for transfers between devices, shards(): whole_block = lax.all_gather(coulomb, ('tm', 'pts'), axis=0, tiled=True)  4.07 us
    convert_element_type x1, other arithmetic, shards(): scaled = (widened * decay[0][None, :]).astype(jnp.bfloat16)  3.44 us
  transfers between devices with their start and end apart: 2, of which 2 were waited for; matrix products, arithmetic and copies ran while one was open for 19% of the time, Pallas kernels for 0%

profile of v1, /device:TPU:0, one launch (start us, length us, event | category | flops | bytes accessed | tf_op | source)
XLA Modules:
  0.0 150.9 jit_solution(11384973944147587020)
XLA Ops:
  6.5 0.0 all-gather.3.cloned.1.call-start
  6.5 0.7 all-gather.3.cloned.1.call-update
  7.3 0.0 all-gather.5.cloned.1.call-start
  7.3 0.7 all-gather.5.cloned.1.call-update
  8.0 1.2 dynamic_slice.3
  9.3 1.3 multiply_exponential_fusion
  10.6 64.2 %all-gather.3.cloned.1.call-done = bf16[1024,2048]{1,0:T(8,128)(2,1)} async-done(((bf16[32,2048]{1,0:T(8,128)(2,1)}), bf16[1024,2048]{1,0:T(8,128)(2,1)}) %all-gather.3.cloned.1.call-update) | async-done | bytes 4194320 | tf_op jit(solution)/shard_map/all_gather | solution.py:24
  74.8 0.0 copy-start
  74.8 3.4 %multiply_convert_fusion = bf16[1024,2048]{1,0:T(8,128)(2,1)S(1)} fusion(bf16[1024,2048]{1,0:T(8,128)(2,1)} %all-gather.3.cloned.1.call-done, f32[2048]{0:T(1024)S(1)} %multiply_exponential_fusion), kind=kLoop, calls=%fused_computation.1 | loop fusion | flops 6291456 | bytes 8396800 | tf_op jit(solution)/shard_map/convert_element_type | solution.py:25
  78.2 0.0 copy-done
  78.2 3.5 %fusion = f32[1024,1024]{1,0:T(8,128)S(1)} fusion(bf16[1024,2048]{1,0:T(8,128)(2,1)S(1)} %multiply_convert_fusion, bf16[1024,2048]{1,0:T(8,128)(2,1)S(1)} %copy-done), kind=kOutput, calls=%fused_computation.4 | convolution fusion | flops 3221225472 | bytes 10485760 | tf_op jit(solution)/shard_map/dot_general | solution.py:13
  81.7 1.3 fusion.3
  83.0 0.1 slice_bitcast_fusion.3
  83.2 0.3 pad_maximum_fusion
  83.4 30.4 %all_to_all.5 = bf16[4,1,256,1024]{2,3,1,0:T(8,128)(2,1)S(1)} all-to-all(bf16[4,1,256,1024]{2,3,1,0:T(8,128)(2,1)S(1)} %pad_maximum_fusion), channel_id=1, replica_groups=mesh['tm'=4,'pts'=8] {'tm'}, dimensions={0} | all-to-all | bytes 4194304 | tf_op jit(solution)/shard_map/all_to_all | solution.py:31
  113.8 0.0 copy-start.1
  113.8 0.0 copy-start.2
  113.8 0.0 copy-start.3
  113.8 2.4 %copy.8 = bf16[4,1,256,1024]{3,2,0,1:T(8,128)(2,1)} copy(bf16[4,1,256,1024]{2,3,1,0:T(8,128)(2,1)S(1)} %all_to_all.5) | data formatting | bytes 4194304 | tf_op jit(solution)/shard_map/all_to_all | solution.py:31
  116.2 3.2 %copy.9 = bf16[1,4,256,1024]{3,1,2,0:T(4,128)(2,1)S(1)} copy(bf16[1,4,256,1024]{3,2,1,0:T(8,128)(2,1)} %bitcast.22) | data formatting | bytes 4194304
  119.4 0.0 copy-done.1
  119.4 0.0 copy-done.2
  119.4 0.0 copy-done.3
  119.4 5.1 %convolution_convert_fusion = bf16[8,262144]{1,0:T(8,128)(2,1)} fusion(bf16[4,262144]{1,0:T(4,128)(2,1)S(1)} %bitcast.21, f32[4]{0:T(128)S(1)} %copy-done.1, f32[8]{0:T(128)S(1)} %copy-done.2, f32[4]{0:T(128)S(1)} %copy-done.3), kind=kOutput, calls=%fused_computation | convolution fusion | flops 102760512 | bytes 6291520 | tf_op jit(solution)/shard_map/dot_general | solution.py:37
  124.5 6.0 %reshape.16 = bf16[2048,1024]{1,0:T(8,128)(2,1)} reshape(bf16[8,262144]{1,0:T(8,128)(2,1)} %convolution_convert_fusion) | data formatting | bytes 8388608 | tf_op jit(solution)/shard_map/reshape | solution.py:38
  130.6 4.1 %all-gather.5.cloned.1.call-done = bf16[1024,1024]{1,0:T(8,128)(2,1)} async-done(((bf16[32,1024]{1,0:T(8,128)(2,1)}), bf16[1024,1024]{1,0:T(8,128)(2,1)}) %all-gather.5.cloned.1.call-update) | async-done | bytes 2097168 | tf_op jit(solution)/shard_map/all_gather | solution.py:39
  134.7 9.4 %convolution_convert_fusion.1 = bf16[2048,1024]{1,0:T(8,128)(2,1)} fusion(bf16[2048,1024]{1,0:T(8,128)(2,1)} %reshape.16, bf16[1024,1024]{1,0:T(8,128)(2,1)} %all-gather.5.cloned.1.call-done), kind=kOutput, calls=%fused_computation.3 | convolution fusion | flops 4297064448 | bytes 10485760 | tf_op jit(solution)/shard_map/dot_general | solution.py:40
Async XLA Ops:
  6.5 68.2 %all-gather.3.cloned.1.call-start = ((), (), s32[]{:S(2)}) async-start(), calls=%async_computation.1 | async-start | bytes 4325376 | tf_op jit(solution)/shard_map/all_gather | solution.py:24
  7.3 127.4 %all-gather.5.cloned.1.call-start = ((), (), s32[]{:S(2)}) async-start(), calls=%async_computation.2 | async-start | bytes 2162688 | tf_op jit(solution)/shard_map/all_gather | solution.py:39
  74.8 3.5 %copy-start = (bf16[1024,2048]{1,0:T(8,128)(2,1)S(1)}, bf16[1024,2048]{1,0:T(8,128)(2,1)}, u32[]{:S(2)}) copy-start(bf16[1024,2048]{1,0:T(8,128)(2,1)} %param.7) | copy-start | bytes 12582916
  113.8 5.6 %copy-start.1 = (f32[4]{0:T(128)S(1)}, f32[4]{0:T(128)}, u32[]{:S(2)}) copy-start(f32[4]{0:T(128)} %param.10) | copy-start | bytes 52
  113.8 5.6 %copy-start.2 = (f32[8]{0:T(128)S(1)}, f32[8]{0:T(128)}, u32[]{:S(2)}) copy-start(f32[8]{0:T(128)} %param.12) | copy-start | bytes 100
  113.8 5.6 %copy-start.3 = (f32[4]{0:T(128)S(1)}, f32[4]{0:T(128)}, u32[]{:S(2)}) copy-start(f32[4]{0:T(128)} %param.11) | copy-start | bytes 52
Sparse Core Ops, SparseCore 0:
  10.3 64.3 all-gather.2
  77.7 56.8 all-gather.4
